TPU v7x, 32 devices: a whole 2x2x4 slice. The times are simulated.
32 devices in a mesh: groups: 2 (over x), tensor: 2 (over core), query: 8 (over z, y).
Axes of the slice: x: 2, y: 2, z: 4, core: 2. Of those that a mesh axis runs over, the one named last changes fastest.
Arguments:
- query_tokens: bfloat16 [1024, 1024], P(('groups', 'tensor', 'query')), parts along dimension 0, may hold values from -6 to 6
- ln_gain: float32 [1024], replicated, may hold values from 0.1 to 1.9
- inner_weight: bfloat16 [1024, 65536], P(None, ('tensor', 'query')), may hold values from -0.1875 to 0.1875
- outer_weight: bfloat16 [65536, 1024], P(('tensor', 'query')), may hold values from -0.03125 to 0.03125
- final_gain: float32 [1024], replicated, may hold values from 0.1 to 1.9
- projection: bfloat16 [1024, 128], replicated, may hold values from -0.1875 to 0.1875
- segment_ids: int32 [1024], P('groups'), parts along dimension 0, may hold values from 0 to 31, never falling along the last dimension, each value on 1 to 32 neighbouring positions
- index_vectors: bfloat16 [131072, 128], P(('groups', 'tensor', 'query')), parts along dimension 0, may hold values from -6 to 6
- doc_ids: int32 [131072], P(('groups', 'tensor', 'query')), parts along dimension 0, may hold values from 0 to 127, as said below
Outputs:
- scores: float32 [32, 4096], P(None, ('groups', 'tensor', 'query')), parts along dimension 1
There are 2 independent parts, one for each index of `groups`. A program takes and returns all parts, laid end to end along the dimension named above; an argument that names none is the same for every part. Nothing has to cross between parts.
Inputs may be any that keep to these rules, and one draw needn't show every extreme that they name: `doc_ids`: within each shard of 4096 tokens the slot numbers never fall, start at 0 and leave no slot out up to the shard's largest; some shard uses all 128 slots. `segment_ids`: every query number appears; a query's tokens stand together.
All inputs are finite; a program needn't handle non-finite values.
Results may differ from a plain program's by a relative error of at most 0.0011.
Values may be sent and summed in bfloat16 or wider, within the bound.
No kernel may reach another device: no remote copies, remote signals or barrier semaphores. Data moves between devices by JAX's collectives and lax.ppermute only.
A program may use at most 128 MiB of HBM per device.

v0:
```python
import jax
import jax.numpy as jnp
from jax import lax
from jax.sharding import PartitionSpec as P

DOC_DEV = 128


EPSILON = 1e-06


def rms_rows(values, gain):
    mean_square = jnp.mean(values * values, axis=-1, keepdims=True)
    return values * lax.rsqrt(mean_square + EPSILON) * gain


def project_rows(mixed, final_gain, projection):
    final = rms_rows(mixed, final_gain).astype(jnp.bfloat16)
    projected = jnp.dot(final, projection, preferred_element_type=jnp.float32)
    scaled = projected * lax.rsqrt(jnp.sum(projected * projected, axis=-1, keepdims=True) + EPSILON)
    return scaled.astype(jnp.bfloat16)


def score_block(totals, query_rows, segment_rows, index_vectors, doc_ids, present):
    sims = jnp.einsum("jp,tp->jt", index_vectors, query_rows, preferred_element_type=jnp.float32)
    best = jax.ops.segment_max(sims, doc_ids, num_segments=totals.shape[1])
    best = jnp.where(present[:, None], best, 0.0)
    member = (segment_rows[None, :] == lax.iota(jnp.int32, totals.shape[0])[:, None]).astype(
        jnp.float32
    )
    return totals + jnp.einsum("qt,dt->qd", member, best, precision=lax.Precision.HIGHEST)


def score_rows(totals, query_rows, segment_rows, index_vectors, doc_ids, present):
    count_rows = query_rows.shape[0]
    if count_rows > 512 and count_rows % 512 == 0:
        blocks = count_rows // 512

        def block_step(carry, inputs):
            return (score_block(carry, inputs[0], inputs[1], index_vectors, doc_ids, present), None)

        stacked = (
            query_rows.reshape(blocks, 512, query_rows.shape[1]),
            segment_rows.reshape(blocks, 512),
        )
        totals, unused = lax.scan(block_step, totals, stacked)
        return totals
    return score_block(totals, query_rows, segment_rows, index_vectors, doc_ids, present)


def on_device(
    query_tokens,
    ln_gain,
    inner_weight,
    outer_weight,
    final_gain,
    projection,
    segment_ids,
    index_vectors,
    doc_ids,
):
    queries = segment_ids.shape[0] // 16
    present = jnp.any(doc_ids[:, None] == lax.iota(jnp.int32, DOC_DEV)[None, :], axis=0)
    empty = jnp.zeros((queries, DOC_DEV), jnp.float32)
    gathered = lax.all_gather(query_tokens, ("tensor", "query"), axis=0, tiled=True)
    normed = rms_rows(gathered.astype(jnp.float32), ln_gain).astype(jnp.bfloat16)
    hidden = jnp.maximum(
        jnp.dot(normed, inner_weight, preferred_element_type=jnp.float32), 0.0
    ).astype(jnp.bfloat16)
    own_out = lax.psum_scatter(
        jnp.dot(hidden, outer_weight, preferred_element_type=jnp.float32),
        ("tensor", "query"),
        scatter_dimension=0,
        tiled=True,
    )
    own_vectors = project_rows(query_tokens.astype(jnp.float32) + own_out, final_gain, projection)
    totals = score_rows(
        empty,
        lax.all_gather(own_vectors, ("tensor", "query"), axis=0, tiled=True),
        segment_ids,
        index_vectors,
        doc_ids,
        present,
    )
    lengths = jnp.sum(
        (segment_ids[None, :] == lax.iota(jnp.int32, queries)[:, None]).astype(jnp.float32), axis=1
    )
    return totals / lengths[:, None]


def solution(mesh):
    return jax.shard_map(
        on_device,
        mesh=mesh,
        in_specs=(
            P(("groups", "tensor", "query"), None),
            P(),
            P(None, ("tensor", "query")),
            P(("tensor", "query"), None),
            P(),
            P(),
            P("groups"),
            P(("groups", "tensor", "query"), None),
            P(("groups", "tensor", "query")),
        ),
        out_specs=P(None, ("groups", "tensor", "query")),
        check_vma=False,
    )
```

profile of v0, /device:TPU:1, one launch (start us, length us, event | category | flops | bytes accessed | tf_op | source)
XLA Modules:
  0.0 204.2 jit_solution(15623690360071753148)
XLA Ops:
  6.5 0.0 copy-start
  6.5 0.0 all-gather.2.cloned.1.call-start
  6.5 0.7 all-gather.2.cloned.1.call-update
  7.3 0.0 reduce-scatter.2.cloned.1.call-start
  7.3 42.6 %all-gather.2.cloned.1.call-done = bf16[512,1024]{1,0:T(8,128)(2,1)} async-done(((bf16[32,1024]{1,0:T(8,128)(2,1)}), bf16[512,1024]{1,0:T(8,128)(2,1)}) %all-gather.2.cloned.1.call-update) | async-done | bytes 1048592 | tf_op jit(solution)/shard_map/all_gather | solution.py:65
  49.9 1.5 fusion.2
  51.4 0.0 copy-start.4
  51.4 0.0 copy-start.3
  51.4 0.0 copy-start.1
  51.5 0.0 copy-start.2
  51.5 0.0 copy-start.5
  51.5 16.4 %fusion.18 = f32[512,1024]{1,0:T(8,128)} fusion(bf16[4096,1024]{1,0:T(8,128)(2,1)} %param.12, bf16[1024,4096]{1,0:T(8,128)(2,1)} %param.11, bf16[512,1024]{1,0:T(8,128)(2,1)} %all-gather.2.cloned.1.call-done, f32[1024]{0:T(1024)} %param.10, f32[512]{0:T(512)S(1)} %add_rsqrt_fusion), kind=kOutput, calls=%fused_computation.33 | convolution fusion | flops 8596226048 | bytes 19929088 | tf_op jit(solution)/shard_map/dot_general | solution.py:71
  67.9 0.0 reduce-scatter.2.cloned.1.call-update
  67.9 0.0 copy-done.4
  67.9 0.1 convert_reduce_fusion
  68.0 0.0 copy-done.3
  68.0 1.9 fusion.5
  69.9 56.7 %reduce-scatter.2.cloned.1.call-done = f32[32,1024]{1,0:T(8,128)} async-done(((f32[512,1024]{1,0:T(8,128)}), f32[32,1024]{1,0:T(8,128)}) %reduce-scatter.2.cloned.1.call-update) | async-done | bytes 131088 | tf_op jit(solution)/shard_map/reduce_scatter | solution.py:70
  126.6 0.0 copy-done.1
  126.6 1.0 multiply_reduce_fusion
  127.6 0.0 copy-done.2
  127.7 0.0 copy-done.5
  127.7 1.2 multiply_reduce_fusion.1
  128.9 0.1 multiply_convert_fusion.2
  129.0 33.3 %all_gather.7 = bf16[512,128]{1,0:T(8,128)(2,1)S(1)} all-gather(bf16[32,128]{1,0:T(8,128)(2,1)S(1)} %multiply_convert_fusion.2), channel_id=1, replica_groups=mesh['groups'=2,'tensor'=2,'query'=8] {'tensor','query'}, dimensions={0}, use_global_device_ids=true | all-gather | bytes 139264 | tf_op jit(solution)/shard_map/all_gather | solution.py:79
  162.3 0.0 copy-done
  162.3 4.5 %fusion.19 = f32[512,4096]{0,1:T(8,128)} fusion(bf16[512,128]{1,0:T(8,128)(2,1)S(1)} %all_gather.7, bf16[4096,128]{1,0:T(8,128)(2,1)S(1)} %copy-done), kind=kOutput, calls=%fused_computation.34 | convolution fusion | flops 536870912 | bytes 9568256 | tf_op jit(solution)/shard_map/jp,tp->jt/dot_general | solution.py:25
  166.8 29.6 %scatter_custom_fusion = f32[128,512]{1,0:T(8,128)S(1)} fusion(s32[4096]{0:T(1024)S(1)} %copy-done.3, f32[512,4096]{0,1:T(8,128)} %fusion.19, f32[]{:T(128)} %constant.6.clone.1), kind=kCustom, calls=%fused_computation.1 | custom fusion | flops 2097152 | bytes 8650756 | tf_op jit(solution)/shard_map/scatter-max | solution.py:26
  196.4 0.9 convolution_divide_fusion
  (3 shorter events, 0.0 us)
Async XLA Ops:
  6.5 155.8 %copy-start = (bf16[4096,128]{1,0:T(8,128)(2,1)S(1)}, bf16[4096,128]{1,0:T(8,128)(2,1)}, u32[]{:S(2)}) copy-start(bf16[4096,128]{1,0:T(8,128)(2,1)} %param.16) | copy-start | bytes 3145732
  6.5 43.4 %all-gather.2.cloned.1.call-start = ((), (), s32[]{:S(2)}) async-start(), calls=%async_computation.1 | async-start | bytes 1114112 | tf_op jit(solution)/shard_map/all_gather | solution.py:65
  7.3 119.3 %reduce-scatter.2.cloned.1.call-start = ((), (), s32[]{:S(2)}) async-start(), calls=%async_computation.2 | async-start | bytes 2228224 | tf_op jit(solution)/shard_map/reduce_scatter | solution.py:70
  51.4 16.5 %copy-start.4 = (s32[512]{0:T(512)S(1)}, s32[512]{0:T(512)}, u32[]{:S(2)}) copy-start(s32[512]{0:T(512)} %param.15) | copy-start | bytes 6148
  51.4 16.6 %copy-start.3 = (s32[4096]{0:T(1024)S(1)}, s32[4096]{0:T(1024)}, u32[]{:S(2)}) copy-start(s32[4096]{0:T(1024)} %param.17) | copy-start | bytes 49156
  51.4 75.2 %copy-start.1 = (bf16[32,1024]{1,0:T(8,128)(2,1)S(1)}, bf16[32,1024]{1,0:T(8,128)(2,1)}, u32[]{:S(2)}) copy-start(bf16[32,1024]{1,0:T(8,128)(2,1)} %param.9) | copy-start | bytes 196612
  51.5 76.2 %copy-start.2 = (bf16[1024,128]{1,0:T(8,128)(2,1)S(1)}, bf16[1024,128]{1,0:T(8,128)(2,1)}, u32[]{:S(2)}) copy-start(bf16[1024,128]{1,0:T(8,128)(2,1)} %param.14) | copy-start | bytes 786436
  51.5 76.2 %copy-start.5 = (f32[1024]{0:T(1024)S(1)}, f32[1024]{0:T(1024)}, u32[]{:S(2)}) copy-start(f32[1024]{0:T(1024)} %param.13) | copy-start | bytes 12292
Sparse Core Ops, SparseCore 0:
  9.5 40.3 all-gather.1
  68.0 58.5 reduce-scatter.1
where the time goes:
time: 204 us
  waiting for transfers between devices  100 us (49%)
  other arithmetic  34.2 us (17%)
  blocking collectives  33.3 us (16%)
  matrix products  23.1 us (11%)
  between operations  13.5 us (7%)
    reduce_scatter x1, waiting for transfers between devices, on_device(): lax.psum_scatter(jnp.dot(hidden, outer_weight, preferred_element_type=jnp...  56.7 us
    all_gather x1, waiting for transfers between devices, on_device(): lax.all_gather(query_tokens, ('tensor', 'query'), axis=0, tiled=True)  42.6 us
    all_gather x1, blocking collectives, on_device(): lax.all_gather(own_vectors, ('tensor', 'query'), axis=0, tiled=True)  33.3 us
    another operation x1, other arithmetic, score_block(): best = jax.ops.segment_max(sims, doc_ids, num_segments=totals.shape[1])  29.6 us
    dot_general x1, matrix products, on_device(): jnp.dot(hidden, outer_weight, preferred_element_type=jnp.float32)  16.4 us
    dot_general x1, matrix products, score_block(): jnp.einsum('jp,tp->jt', index_vectors, query_rows, preferred_element_type...  4.47 us
  transfers between devices with their start and end apart: 2, of which 2 were waited for; matrix products, arithmetic and copies ran while one was open for 1% of the time, Pallas kernels for 0%

commit v1 on v0

v1 whole, which is shorter than its diff:
```python
import functools

import jax
import jax.numpy as jnp
from jax import lax
from jax.experimental import pallas as pl
from jax.experimental.pallas import tpu as pltpu
from jax.sharding import PartitionSpec as P

DOC_DEV = 128
EPSILON = 1e-06
RING = ("tensor", "query")
LOW = float("-inf")
VMEM = pl.BlockSpec(memory_space=pltpu.VMEM)
SMEM = pl.BlockSpec(memory_space=pltpu.SMEM)


def masks_of(cores, places):
    near = 2 if places % 2 == 0 else 1
    far = [k * near for k in range(places // near)]
    side = [0, 1] if near == 2 else [0]
    core = [c * places for c in range(cores)]
    return far, side, core


def hop(value, mask, count):
    return lax.ppermute(value, RING, [(i, i ^ mask) for i in range(count)])


def gather_rows(rows, far, side, core, count):
    for masks in (far, side, core):
        rows = jnp.concatenate([rows] + [hop(rows, m, count) for m in masks[1:]], axis=0)
    return rows


def norm_kernel(x_ref, gain_ref, out_ref):
    x = x_ref[...].astype(jnp.float32)
    mean_square = jnp.mean(x * x, axis=-1, keepdims=True)
    out_ref[...] = (x * lax.rsqrt(mean_square + EPSILON) * gain_ref[...]).astype(jnp.bfloat16)


def norm_rows(x, gain):
    return pl.pallas_call(
        norm_kernel, out_shape=jax.ShapeDtypeStruct(x.shape, jnp.bfloat16), in_specs=[VMEM, VMEM], out_specs=VMEM
    )(x, gain[None, :])


def ff_kernel(x_ref, inner_ref, outer_ref, keep_ref, send_ref, sum_ref):
    step = pl.program_id(0)
    hidden = jnp.maximum(jnp.dot(x_ref[...], inner_ref[...], preferred_element_type=jnp.float32), 0.0)
    part = jnp.dot(hidden.astype(jnp.bfloat16), outer_ref[...], preferred_element_type=jnp.float32)

    @pl.when(step == 0)
    def first():
        sum_ref[...] = part

    @pl.when(step > 0)
    def later():
        sum_ref[...] += part

    @pl.when(step == pl.num_programs(0) - 1)
    def last():
        half = keep_ref.shape[0]
        keep_ref[...] = sum_ref[:half, :]
        send_ref[...] = sum_ref[half:, :].astype(jnp.bfloat16)


def feed_forward(x, inner, outer):
    rows, width = x.shape
    units = inner.shape[1]
    tile = min(1024, units)
    half = rows // 2
    return pl.pallas_call(
        ff_kernel,
        grid=(units // tile,),
        in_specs=[
            pl.BlockSpec((rows, width), lambda i: (0, 0)),
            pl.BlockSpec((width, tile), lambda i: (0, i)),
            pl.BlockSpec((tile, width), lambda i: (i, 0)),
        ],
        out_specs=[pl.BlockSpec((half, width), lambda i: (0, 0))] * 2,
        out_shape=[jax.ShapeDtypeStruct((half, width), jnp.float32), jax.ShapeDtypeStruct((half, width), jnp.bfloat16)],
        scratch_shapes=[pltpu.VMEM((rows, width), jnp.float32)],
        compiler_params=pltpu.CompilerParams(vmem_limit_bytes=56 << 20),
        cost_estimate=pl.CostEstimate(
            flops=4 * rows * width * units, bytes_accessed=4 * width * units, transcendentals=0
        ),
    )(x, inner, outer)


def project_kernel(x_ref, own_ref, got_ref, gain_ref, proj_ref, out_ref):
    mixed = x_ref[...].astype(jnp.float32) + own_ref[...]
    for k in range(got_ref.shape[0]):
        mixed = mixed + got_ref[k].astype(jnp.float32)
    mean_square = jnp.mean(mixed * mixed, axis=-1, keepdims=True)
    final = (mixed * lax.rsqrt(mean_square + EPSILON) * gain_ref[...]).astype(jnp.bfloat16)
    p = jnp.dot(final, proj_ref[...], preferred_element_type=jnp.float32)
    out_ref[...] = (p * lax.rsqrt(jnp.sum(p * p, axis=-1, keepdims=True) + EPSILON)).astype(jnp.bfloat16)


def project_rows(x, own, got, gain, projection):
    return pl.pallas_call(
        project_kernel,
        out_shape=jax.ShapeDtypeStruct((x.shape[0], projection.shape[1]), jnp.bfloat16),
        in_specs=[VMEM] * 5,
        out_specs=VMEM,
    )(x, own, got, gain[None, :], projection)


def score_kernel(bounds, q_ref, seg_ref, index_ref, keep_ref, out_ref, run_ref, best_ref):
    docs, tokens, slots, queries = index_ref.shape[0], q_ref.shape[0], best_ref.shape[0], out_ref.shape[0]
    rows = 256 if docs % 256 == 0 else 8
    run_ref[0:8, :] = jnp.full((8, tokens), LOW, jnp.float32)
    q = q_ref[...]

    def tile(i, run):
        base = pl.multiple_of(i * rows, rows)
        sims = lax.dot_general(
            index_ref[pl.ds(base, rows), :], q, (((1,), (1,)), ((), ())), preferred_element_type=jnp.float32
        )
        keep = keep_ref[pl.ds(base, rows), :]
        for g in range(0, rows, 8):
            same = jnp.concatenate([keep[g : g + 8, :]] * (tokens // keep.shape[1]), axis=1)
            run = jnp.maximum(sims[g : g + 8, :], run + same)
            run_ref[pl.ds(base + 8 + g, 8), :] = run
        return run

    lax.fori_loop(0, docs // rows, tile, jnp.full((8, tokens), LOW, jnp.float32))
    sub = lax.broadcasted_iota(jnp.int32, (8, tokens), 0)

    def octet(o, carry):
        lines = []
        for k in range(8):
            start, end = bounds[o * 8 + k], bounds[o * 8 + k + 1]
            last = pl.multiple_of((jnp.maximum(end - 1, 0) // 8) * 8, 8)
            row = sub + last
            now = jnp.where((row >= start) & (row < end), run_ref[pl.ds(last + 8, 8), :], LOW)
            ago = jnp.where((row - 8 >= start) & (row - 8 < end), run_ref[pl.ds(last, 8), :], LOW)
            line = jnp.max(jnp.maximum(now, ago), axis=0, keepdims=True)
            lines.append(jnp.where(end > start, line, 0.0))
        best_ref[pl.ds(pl.multiple_of(o * 8, 8), 8), :] = jnp.concatenate(lines, axis=0)
        return carry

    lax.fori_loop(0, slots // 8, octet, 0)
    member = (lax.broadcasted_iota(jnp.int32, (queries, tokens), 0) == seg_ref[...]).astype(jnp.float32)
    lengths = jnp.sum(member, axis=1, keepdims=True)
    totals = lax.dot_general(
        member,
        best_ref[...],
        (((1,), (1,)), ((), ())),
        precision=lax.Precision.HIGHEST,
        preferred_element_type=jnp.float32,
    )
    out_ref[...] = totals / lengths


def slot_bounds(doc_ids):
    ids = lax.iota(jnp.int32, DOC_DEV + 1)
    return jnp.sum((doc_ids[None, :] < ids[:, None]).astype(jnp.int32), axis=1)


def same_as_before(doc_ids):
    before = jnp.concatenate([jnp.full((8,), -1, jnp.int32), doc_ids[:-8]])
    same = jnp.where(before == doc_ids, 0.0, LOW).astype(jnp.float32)
    return jnp.broadcast_to(same[:, None], (doc_ids.shape[0], 128))


def score_rows(vectors, segments, index_vectors, bounds, same, queries):
    tokens, docs = vectors.shape[0], index_vectors.shape[0]
    block = 512 if tokens % 512 == 0 else tokens
    return pl.pallas_call(
        score_kernel,
        out_shape=jax.ShapeDtypeStruct((queries, DOC_DEV), jnp.float32),
        in_specs=[SMEM, VMEM, VMEM, VMEM, VMEM],
        out_specs=VMEM,
        scratch_shapes=[pltpu.VMEM((docs + 8, tokens), jnp.float32), pltpu.VMEM((DOC_DEV, tokens), jnp.float32)],
        compiler_params=pltpu.CompilerParams(vmem_limit_bytes=56 << 20),
        cost_estimate=pl.CostEstimate(flops=2 * tokens * docs * 128, bytes_accessed=docs * 256, transcendentals=0),
    )(bounds, vectors, segments[None, :], index_vectors, same)


def on_device(
    cores,
    places,
    query_tokens,
    ln_gain,
    inner_weight,
    outer_weight,
    final_gain,
    projection,
    segment_ids,
    index_vectors,
    doc_ids,
):
    count = cores * places
    own = query_tokens.shape[0]
    queries = segment_ids.shape[0] // 16
    far, side, core = masks_of(cores, places)
    order = jnp.array([c ^ s ^ f for c in core for s in side for f in far], jnp.int32)
    bounds = slot_bounds(doc_ids)
    same = same_as_before(doc_ids)
    segments = segment_ids.reshape(count, own)[order ^ lax.axis_index(RING)].reshape(-1)

    normed = gather_rows(norm_rows(query_tokens, ln_gain), far, side, core, count)
    keep, send = feed_forward(normed, inner_weight, outer_weight)
    keep = keep + hop(send, core[1], count).astype(jnp.float32)
    if len(side) == 2:
        half = keep.shape[0] // 2
        keep = keep[:half] + hop(keep[half:].astype(jnp.bfloat16), side[1], count).astype(jnp.float32)
    send = keep[own:].astype(jnp.bfloat16)
    got = jnp.stack([hop(send[k * own : (k + 1) * own], m, count) for k, m in enumerate(far[1:])])
    own_vectors = project_rows(query_tokens, keep[:own], got, final_gain, projection)
    vectors = gather_rows(own_vectors, far, side, core, count)
    return score_rows(vectors, segments, index_vectors, bounds, same, queries)


def solution(mesh):
    return jax.shard_map(
        functools.partial(on_device, mesh.shape["tensor"], mesh.shape["query"]),
        mesh=mesh,
        in_specs=(
            P(("groups", "tensor", "query"), None),
            P(),
            P(None, ("tensor", "query")),
            P(("tensor", "query"), None),
            P(),
            P(),
            P("groups"),
            P(("groups", "tensor", "query"), None),
            P(("groups", "tensor", "query")),
        ),
        out_specs=P(None, ("groups", "tensor", "query")),
        check_vma=False,
    )
```

time: 204 us -> 86.6 us (0.42)
  waiting for transfers between devices: 100 us -> 24.3 us
  blocking collectives: 33.3 us -> 0 us
  other arithmetic: 34.2 us -> 4.68 us
  Pallas kernels: 0 us -> 26.1 us
  starting transfers between devices: 0.04 us -> 24.3 us
  matrix products: 23.1 us -> 0 us
  between operations: 13.5 us -> 0.12 us
  local copies, waits for them, and re-layouts: 0.04 us -> 6.76 us
    reduce_scatter x1 -> x0, waiting for transfers between devices: 56.7 us -> none  [on_device(): lax.psum_scatter(jnp.dot(hidden, outer_weight, preferred_element_type=jnp...]
    all_gather x1 -> x0, waiting for transfers between devices: 42.6 us -> none  [on_device(): lax.all_gather(query_tokens, ('tensor', 'query'), axis=0, tiled=True)]
    all_gather x1 -> x0, blocking collectives: 33.3 us -> none  [on_device(): lax.all_gather(own_vectors, ('tensor', 'query'), axis=0, tiled=True)]
    another operation x1 -> x2, other arithmetic: 29.6 us -> 0.78 us  [the longest x1 0.71 us: on_device(): jnp.stack([hop(send[k * own:(k + 1) * own], m, count) for k, m in enumera...]
    pallas_call x0 -> x4, Pallas kernels: none -> 26.1 us  [the longest x1 14.5 us: feed_forward(): pl.pallas_call(ff_kernel, grid=(units // tile,), in_specs=[pl.BlockSpec((...]
    ppermute x0 -> x15, waiting for transfers between devices: none -> 24.3 us  [hop(): return lax.ppermute(value, RING, [(i, i ^ mask) for i in range(count)])]
    ppermute x0 -> x15, starting transfers between devices: none -> 24.3 us  [hop(): return lax.ppermute(value, RING, [(i, i ^ mask) for i in range(count)])]
    dot_general x4 -> x0, matrix products: 23.1 us -> none  [the longest x1 16.4 us: on_device(): jnp.dot(hidden, outer_weight, preferred_element_type=jnp.float32)]
  transfers between devices with their start and end apart: 2 -> 15, of which waited for: 2 -> 10; matrix products, arithmetic and copies ran while one was open for 1% -> 5% of each run, Pallas kernels for 0% -> 0%
where the time goes in v1:
time: 86.6 us; the launch traced here: 86.2 us
  Pallas kernels  26.1 us (30%)
  starting transfers between devices  24.3 us (28%)
  waiting for transfers between devices  24.3 us (28%)
  local copies, waits for them, and re-layouts  6.76 us (8%)
  other arithmetic  4.68 us (5%)
    ppermute x15, waiting for transfers between devices, hop(): return lax.ppermute(value, RING, [(i, i ^ mask) for i in range(count)])  24.3 us
    ppermute x15, starting transfers between devices, hop(): return lax.ppermute(value, RING, [(i, i ^ mask) for i in range(count)])  24.3 us
    pallas_call x1, Pallas kernels, feed_forward(): pl.pallas_call(ff_kernel, grid=(units // tile,), in_specs=[pl.BlockSpec((...  14.5 us
    pallas_call x1, Pallas kernels, score_rows(): pl.pallas_call(score_kernel, out_shape=jax.ShapeDtypeStruct((queries, DOC...  7.86 us
    unnamed x18, local copies, waits for them, and re-layouts  2.7 us
    pallas_call x1, Pallas kernels, project_rows(): pl.pallas_call(project_kernel, out_shape=jax.ShapeDtypeStruct((x.shape[0]...  2.11 us
    broadcast_in_dim x1, local copies, waits for them, and re-layouts, same_as_before(): return jnp.broadcast_to(same[:, None], (doc_ids.shape[0], 128))  1.96 us
  transfers between devices with their start and end apart: 15, of which 10 were waited for; matrix products, arithmetic and copies ran while one was open for 5% of the time, Pallas kernels for 0%

profile of v1, /device:TPU:1, one launch (start us, length us, event | category | flops | bytes accessed | tf_op | source)
XLA Modules:
  0.0 86.2 jit_solution(14422767915586246132)
XLA Ops:
  0.0 1.6 %shard_map.100 = bf16[32,1024]{1,0:T(8,128)(2,1)} custom-call(bf16[32,1024]{1,0:T(8,128)(2,1)} %x_ref.3, f32[1,1024]{1,0:T(1,128)} %bitcast.11), custom_call_target="tpu_custom_call" | custom-call | tf_op jit(solution)/shard_map/pallas_call | solution.py:43
  1.6 2.1 %collective-permute-start = (bf16[32,1024]{1,0:T(8,128)(2,1)}, bf16[32,1024]{1,0:T(8,128)(2,1)S(1)}, u32[]{:S(2)}, u32[]{:S(2)}) collective-permute-start(bf16[32,1024]{1,0:T(8,128)(2,1)} %shard_map.100), channel_id=1, source_target_pairs={{0,2},{1,3},{2,0},{3,1},{4,6},{5,7},{6,4},{7,5},{8,10},{9,11},{10,... | collective-permute-start | bytes 196616 | tf_op jit(solution)/shard_map/ppermute | solution.py:27
  3.7 2.3 %collective-permute-start.1 = (bf16[32,1024]{1,0:T(8,128)(2,1)}, bf16[32,1024]{1,0:T(8,128)(2,1)S(1)}, u32[]{:S(2)}, u32[]{:S(2)}) collective-permute-start(bf16[32,1024]{1,0:T(8,128)(2,1)} %shard_map.100), channel_id=1, source_target_pairs={{0,4},{1,5},{2,6},{3,7},{4,0},{5,1},{6,2},{7,3},{8,12},{9,13},{10,... | collective-permute-start | bytes 196616 | tf_op jit(solution)/shard_map/ppermute | solution.py:27
  6.0 0.0 collective-permute-start.2
  6.0 0.9 %constant_dynamic-update-slice_fusion.4 = (bf16[256,1024]{1,0:T(8,128)(2,1)S(1)}, bf16[512,1024]{1,0:T(8,128)(2,1)S(1)}) fusion(bf16[32,1024]{1,0:T(8,128)(2,1)} %shard_map.100), kind=kLoop, calls=%fused_computation.12 | loop fusion | bytes 196608
  6.9 0.0 collective-permute-done
  6.9 1.6 %collective-permute-done.1 = bf16[32,1024]{1,0:T(8,128)(2,1)S(1)} collective-permute-done((bf16[32,1024]{1,0:T(8,128)(2,1)}, bf16[32,1024]{1,0:T(8,128)(2,1)S(1)}, u32[]{:S(2)}, u32[]{:S(2)}) %collective-permute-start.1) | collective-permute-done | bytes 65568 | tf_op jit(solution)/shard_map/ppermute | solution.py:27
  8.5 2.7 %collective-permute-done.2 = bf16[32,1024]{1,0:T(8,128)(2,1)S(1)} collective-permute-done((bf16[32,1024]{1,0:T(8,128)(2,1)}, bf16[32,1024]{1,0:T(8,128)(2,1)S(1)}, u32[]{:S(2)}, u32[]{:S(2)}) %collective-permute-start.2) | collective-permute-done | bytes 65568 | tf_op jit(solution)/shard_map/ppermute | solution.py:27
  11.2 0.9 pad_maximum_fusion
  12.1 1.3 %collective-permute-start.3 = (bf16[128,1024]{1,0:T(8,128)(2,1)S(1)}, bf16[128,1024]{1,0:T(8,128)(2,1)S(1)}, u32[]{:S(2)}, u32[]{:S(2)}) collective-permute-start(bf16[128,1024]{1,0:T(8,128)(2,1)S(1)} %pad_maximum_fusion), channel_id=1, source_target_pairs={{0,1},{1,0},{2,3},{3,2},{4,5},{5,4},{6,7},{7,6},{8,9},{9,8},{10,11... | collective-permute-start | bytes 786440 | tf_op jit(solution)/shard_map/ppermute | solution.py:27
  13.4 4.3 %collective-permute-done.3 = bf16[128,1024]{1,0:T(8,128)(2,1)S(1)} collective-permute-done((bf16[128,1024]{1,0:T(8,128)(2,1)S(1)}, bf16[128,1024]{1,0:T(8,128)(2,1)S(1)}, u32[]{:S(2)}, u32[]{:S(2)}) %collective-permute-start.3) | collective-permute-done | bytes 262176 | tf_op jit(solution)/shard_map/ppermute | solution.py:27
  17.7 3.2 %collective-permute-start.4 = (bf16[256,1024]{1,0:T(8,128)(2,1)S(1)}, bf16[256,1024]{1,0:T(8,128)(2,1)S(1)}, u32[]{:S(2)}, u32[]{:S(2)}) collective-permute-start(bf16[256,1024]{1,0:T(8,128)(2,1)S(1)} %get-tuple-element.14), channel_id=1, source_target_pairs={{0,8},{1,9},{2,10},{3,11},{4,12},{5,13},{6,14},{7,15},{8,0},{9,1},... | collective-permute-start | bytes 1572872 | tf_op jit(solution)/shard_map/ppermute | solution.py:27
  21.0 1.5 %collective-permute-done.4 = bf16[256,1024]{1,0:T(8,128)(2,1)S(1)} collective-permute-done((bf16[256,1024]{1,0:T(8,128)(2,1)S(1)}, bf16[256,1024]{1,0:T(8,128)(2,1)S(1)}, u32[]{:S(2)}, u32[]{:S(2)}) %collective-permute-start.4) | collective-permute-done | bytes 524320 | tf_op jit(solution)/shard_map/ppermute | solution.py:27
  22.6 0.0 copy-start.2
  22.6 1.0 %copy-done.2 = bf16[512,1024]{1,0:T(8,128)(2,1)} copy-done((bf16[512,1024]{1,0:T(8,128)(2,1)}, bf16[512,1024]{1,0:T(8,128)(2,1)S(1)}, u32[]{:S(2)}) %copy-start.2) | copy-done | bytes 1048600
  23.5 14.5 %shard_map.101 = (f32[256,1024]{1,0:T(8,128)}, bf16[256,1024]{1,0:T(8,128)(2,1)}) custom-call(bf16[512,1024]{1,0:T(8,128)(2,1)} %copy-done.2, bf16[1024,4096]{1,0:T(8,128)(2,1)} %inner_ref.1, bf16[4096,1024]{1,0:T(8,128)(2,1)} %outer_ref.1), custom_call_target="tpu_custom_call" | custom-call | flops 8589934592 | bytes 16777216 | tf_op jit(solution)/shard_map/pallas_call | solution.py:73
  38.1 0.0 copy-start.4
  38.1 0.0 copy-start.1
  38.1 0.4 collective-permute-start.5
  38.5 1.7 %collective-permute-done.5 = bf16[256,1024]{1,0:T(8,128)(2,1)S(1)} collective-permute-done((bf16[256,1024]{1,0:T(8,128)(2,1)}, bf16[256,1024]{1,0:T(8,128)(2,1)S(1)}, u32[]{:S(2)}, u32[]{:S(2)}) %collective-permute-start.5) | collective-permute-done | bytes 524320 | tf_op jit(solution)/shard_map/ppermute | solution.py:27
  40.2 0.0 copy-start.3
  40.2 1.4 %convert_add_fusion = f32[256,1024]{1,0:T(8,128)S(1)} fusion(f32[256,1024]{1,0:T(8,128)} %get-tuple-element.7, bf16[256,1024]{1,0:T(8,128)(2,1)S(1)} %collective-permute-done.5), kind=kLoop, calls=%fused_computation.3 | loop fusion | flops 524288 | bytes 2621440 | tf_op jit(solution)/shard_map/add | solution.py:206
  41.6 1.3 %collective-permute-start.6 = (bf16[128,1024]{1,0:T(8,128)(2,1)S(1)}, bf16[128,1024]{1,0:T(8,128)(2,1)S(1)}, u32[]{:S(2)}, u32[]{:S(2)}) collective-permute-start(bf16[128,1024]{1,0:T(8,128)(2,1)S(1)} %slice.44), channel_id=1, source_target_pairs={{0,1},{1,0},{2,3},{3,2},{4,5},{5,4},{6,7},{7,6},{8,9},{9,8},{10,11... | collective-permute-start | bytes 786440 | tf_op jit(solution)/shard_map/ppermute | solution.py:27
  42.9 0.0 copy-done.4
  42.9 0.0 copy-done.1
  43.0 0.1 fusion
  43.0 6.2 %collective-permute-done.6 = bf16[128,1024]{1,0:T(8,128)(2,1)S(1)} collective-permute-done((bf16[128,1024]{1,0:T(8,128)(2,1)S(1)}, bf16[128,1024]{1,0:T(8,128)(2,1)S(1)}, u32[]{:S(2)}, u32[]{:S(2)}) %collective-permute-start.6) | collective-permute-done | bytes 262176 | tf_op jit(solution)/shard_map/ppermute | solution.py:27
  49.2 0.1 fusion.1
  49.3 0.5 collective-permute-start.7
  49.8 1.4 %collective-permute-start.8 = (bf16[32,1024]{1,0:T(8,128)(2,1)S(1)}, bf16[32,1024]{1,0:T(8,128)(2,1)S(1)}, u32[]{:S(2)}, u32[]{:S(2)}) collective-permute-start(bf16[32,1024]{1,0:T(8,128)(2,1)S(1)} %get-tuple-element.13), channel_id=1, source_target_pairs={{0,4},{1,5},{2,6},{3,7},{4,0},{5,1},{6,2},{7,3},{8,12},{9,13},{10,... | collective-permute-start | bytes 196616 | tf_op jit(solution)/shard_map/ppermute | solution.py:27
  51.2 1.7 %collective-permute-start.9 = (bf16[32,1024]{1,0:T(8,128)(2,1)S(1)}, bf16[32,1024]{1,0:T(8,128)(2,1)S(1)}, u32[]{:S(2)}, u32[]{:S(2)}) collective-permute-start(bf16[32,1024]{1,0:T(8,128)(2,1)S(1)} %get-tuple-element.12), channel_id=1, source_target_pairs={{0,6},{1,7},{2,4},{3,5},{4,2},{5,3},{6,0},{7,1},{8,14},{9,15},{10,... | collective-permute-start | bytes 196616 | tf_op jit(solution)/shard_map/ppermute | solution.py:27
  52.9 0.9 %convert_reduce_fusion.bounds = s32[129]{0:T(256)} fusion(s32[4096]{0:T(1024)S(1)} %copy-done.1), kind=kLoop, calls=%fused_computation.1 | loop fusion | flops 1585023 | bytes 16900 | tf_op jit(solution)/shard_map/reduce_sum | solution.py:159
  53.8 0.0 copy-done.3
  53.8 0.1 reshape.5
  53.9 0.7 slice.38.own_ref
  54.5 0.0 collective-permute-done.7
  54.5 0.0 collective-permute-done.8
  54.5 2.4 %collective-permute-done.9 = bf16[32,1024]{1,0:T(8,128)(2,1)S(1)} collective-permute-done((bf16[32,1024]{1,0:T(8,128)(2,1)S(1)}, bf16[32,1024]{1,0:T(8,128)(2,1)S(1)}, u32[]{:S(2)}, u32[]{:S(2)}) %collective-permute-start.9) | collective-permute-done | bytes 65568 | tf_op jit(solution)/shard_map/ppermute | solution.py:27
  57.0 0.7 pad_maximum_fusion.1.got_ref
  57.7 2.1 %shard_map.102 = bf16[32,128]{1,0:T(8,128)(2,1)} custom-call(bf16[32,1024]{1,0:T(8,128)(2,1)} %x_ref.3, f32[32,1024]{1,0:T(8,128)} %slice.38.own_ref, bf16[3,32,1024]{2,1,0:T(8,128)(2,1)} %pad_maximum_fusion.1.got_ref, f32[1,1024]{1,0:T(1,128)} %bitcast.10, bf16[1024,128]{1,0:T(8,128)(2,1)} %proj_ref.1), custom_call_target="tpu_custom_call" | custom-call | tf_op jit(solution)/shard_map/pallas_call | solution.py:102
  59.8 0.8 collective-permute-start.10
  60.5 1.1 %collective-permute-start.11 = (bf16[32,128]{1,0:T(8,128)(2,1)}, bf16[32,128]{1,0:T(8,128)(2,1)S(1)}, u32[]{:S(2)}, u32[]{:S(2)}) collective-permute-start(bf16[32,128]{1,0:T(8,128)(2,1)} %shard_map.102), channel_id=1, source_target_pairs={{0,4},{1,5},{2,6},{3,7},{4,0},{5,1},{6,2},{7,3},{8,12},{9,13},{10,... | collective-permute-start | bytes 24584 | tf_op jit(solution)/shard_map/ppermute | solution.py:27
  61.6 1.7 %collective-permute-start.12 = (bf16[32,128]{1,0:T(8,128)(2,1)}, bf16[32,128]{1,0:T(8,128)(2,1)S(1)}, u32[]{:S(2)}, u32[]{:S(2)}) collective-permute-start(bf16[32,128]{1,0:T(8,128)(2,1)} %shard_map.102), channel_id=1, source_target_pairs={{0,6},{1,7},{2,4},{3,5},{4,2},{5,3},{6,0},{7,1},{8,14},{9,15},{10,... | collective-permute-start | bytes 24584 | tf_op jit(solution)/shard_map/ppermute | solution.py:27
  63.3 0.7 constant_dynamic-update-slice_fusion.15
  64.0 0.0 collective-permute-done.10
  64.1 0.1 collective-permute-done.11
  64.1 2.0 %collective-permute-done.12 = bf16[32,128]{1,0:T(8,128)(2,1)S(1)} collective-permute-done((bf16[32,128]{1,0:T(8,128)(2,1)}, bf16[32,128]{1,0:T(8,128)(2,1)S(1)}, u32[]{:S(2)}, u32[]{:S(2)}) %collective-permute-start.12) | collective-permute-done | bytes 8224 | tf_op jit(solution)/shard_map/ppermute | solution.py:27
  66.1 0.7 pad_maximum_fusion.2
  66.8 1.2 %collective-permute-start.13 = (bf16[128,128]{1,0:T(8,128)(2,1)S(1)}, bf16[128,128]{1,0:T(8,128)(2,1)S(1)}, u32[]{:S(2)}, u32[]{:S(2)}) collective-permute-start(bf16[128,128]{1,0:T(8,128)(2,1)S(1)} %pad_maximum_fusion.2), channel_id=1, source_target_pairs={{0,1},{1,0},{2,3},{3,2},{4,5},{5,4},{6,7},{7,6},{8,9},{9,8},{10,11... | collective-permute-start | bytes 98312 | tf_op jit(solution)/shard_map/ppermute | solution.py:27
  68.1 1.8 %collective-permute-done.13 = bf16[128,128]{1,0:T(8,128)(2,1)S(1)} collective-permute-done((bf16[128,128]{1,0:T(8,128)(2,1)S(1)}, bf16[128,128]{1,0:T(8,128)(2,1)S(1)}, u32[]{:S(2)}, u32[]{:S(2)}) %collective-permute-start.13) | collective-permute-done | bytes 32800 | tf_op jit(solution)/shard_map/ppermute | solution.py:27
  69.9 5.2 %collective-permute-start.14 = (bf16[256,128]{1,0:T(8,128)(2,1)S(1)}, bf16[256,128]{1,0:T(8,128)(2,1)S(1)}, u32[]{:S(2)}, u32[]{:S(2)}) collective-permute-start(bf16[256,128]{1,0:T(8,128)(2,1)S(1)} %get-tuple-element.24), channel_id=1, source_target_pairs={{0,8},{1,9},{2,10},{3,11},{4,12},{5,13},{6,14},{7,15},{8,0},{9,1},... | collective-permute-start | bytes 196616 | tf_op jit(solution)/shard_map/ppermute | solution.py:27
  75.1 0.6 gather_fusion
  75.6 0.7 broadcast_in_dim_reshape.3.seg_ref
  76.3 0.0 collective-permute-done.14
  76.3 0.0 copy-start
  76.3 2.0 %broadcast_in_dim.30.keep_ref = f32[4096,128]{1,0:T(8,128)} broadcast(f32[4096]{0:T(1024)S(1)} %fusion), dimensions={0} | broadcast | bytes 2113536 | tf_op jit(solution)/shard_map/broadcast_in_dim | solution.py:165
  78.3 0.0 copy-done
  78.3 7.9 %shard_map.103 = f32[32,128]{1,0:T(8,128)} custom-call(s32[129]{0:T(256)} %convert_reduce_fusion.bounds, bf16[512,128]{1,0:T(8,128)(2,1)} %copy-done, s32[1,512]{1,0:T(1,128)} %broadcast_in_dim_reshape.3.seg_ref, bf16[4096,128]{1,0:T(8,128)(2,1)} %index_ref.1, f32[4096,128]{1,0:T(8,128)} %broadcast_in_dim.30.keep_ref), custom_call_target="tpu_custom_call" | custom-call | flops 536870912 | bytes 1048576 | tf_op jit(solution)/shard_map/pallas_call | solution.py:171
  (14 shorter events, 0.2 us)
Async XLA Ops:
  1.6 5.3 %collective-permute-start = (bf16[32,1024]{1,0:T(8,128)(2,1)}, bf16[32,1024]{1,0:T(8,128)(2,1)S(1)}, u32[]{:S(2)}, u32[]{:S(2)}) collective-permute-start(bf16[32,1024]{1,0:T(8,128)(2,1)} %shard_map.100), channel_id=1, source_target_pairs={{0,2},{1,3},{2,0},{3,1},{4,6},{5,7},{6,4},{7,5},{8,10},{9,11},{10,... | collective-permute-start | bytes 196616 | tf_op jit(solution)/shard_map/ppermute | solution.py:27
  3.7 4.9 %collective-permute-start.1 = (bf16[32,1024]{1,0:T(8,128)(2,1)}, bf16[32,1024]{1,0:T(8,128)(2,1)S(1)}, u32[]{:S(2)}, u32[]{:S(2)}) collective-permute-start(bf16[32,1024]{1,0:T(8,128)(2,1)} %shard_map.100), channel_id=1, source_target_pairs={{0,4},{1,5},{2,6},{3,7},{4,0},{5,1},{6,2},{7,3},{8,12},{9,13},{10,... | collective-permute-start | bytes 196616 | tf_op jit(solution)/shard_map/ppermute | solution.py:27
  6.0 5.2 %collective-permute-start.2 = (bf16[32,1024]{1,0:T(8,128)(2,1)}, bf16[32,1024]{1,0:T(8,128)(2,1)S(1)}, u32[]{:S(2)}, u32[]{:S(2)}) collective-permute-start(bf16[32,1024]{1,0:T(8,128)(2,1)} %shard_map.100), channel_id=1, source_target_pairs={{0,6},{1,7},{2,4},{3,5},{4,2},{5,3},{6,0},{7,1},{8,14},{9,15},{10,... | collective-permute-start | bytes 196616 | tf_op jit(solution)/shard_map/ppermute | solution.py:27
  12.1 5.6 %collective-permute-start.3 = (bf16[128,1024]{1,0:T(8,128)(2,1)S(1)}, bf16[128,1024]{1,0:T(8,128)(2,1)S(1)}, u32[]{:S(2)}, u32[]{:S(2)}) collective-permute-start(bf16[128,1024]{1,0:T(8,128)(2,1)S(1)} %pad_maximum_fusion), channel_id=1, source_target_pairs={{0,1},{1,0},{2,3},{3,2},{4,5},{5,4},{6,7},{7,6},{8,9},{9,8},{10,11... | collective-permute-start | bytes 786440 | tf_op jit(solution)/shard_map/ppermute | solution.py:27
  17.7 4.8 %collective-permute-start.4 = (bf16[256,1024]{1,0:T(8,128)(2,1)S(1)}, bf16[256,1024]{1,0:T(8,128)(2,1)S(1)}, u32[]{:S(2)}, u32[]{:S(2)}) collective-permute-start(bf16[256,1024]{1,0:T(8,128)(2,1)S(1)} %get-tuple-element.14), channel_id=1, source_target_pairs={{0,8},{1,9},{2,10},{3,11},{4,12},{5,13},{6,14},{7,15},{8,0},{9,1},... | collective-permute-start | bytes 1572872 | tf_op jit(solution)/shard_map/ppermute | solution.py:27
  22.6 1.0 %copy-start.2 = (bf16[512,1024]{1,0:T(8,128)(2,1)}, bf16[512,1024]{1,0:T(8,128)(2,1)S(1)}, u32[]{:S(2)}) copy-start(bf16[512,1024]{1,0:T(8,128)(2,1)S(1)} %constant_dynamic-update-slice_fusion.5.x_ref) | copy-start | bytes 3145732
  38.1 4.9 %copy-start.4 = (s32[16]{0:T(128)S(1)}, s32[16]{0:T(128)}, u32[]{:S(2)}) copy-start(s32[16]{0:T(128)} %constant.24.clone) | copy-start | bytes 196
  38.1 4.9 %copy-start.1 = (s32[4096]{0:T(1024)S(1)}, s32[4096]{0:T(1024)}, u32[]{:S(2)}) copy-start(s32[4096]{0:T(1024)} %param.18) | copy-start | bytes 49156
  38.1 2.1 %collective-permute-start.5 = (bf16[256,1024]{1,0:T(8,128)(2,1)}, bf16[256,1024]{1,0:T(8,128)(2,1)S(1)}, u32[]{:S(2)}, u32[]{:S(2)}) collective-permute-start(bf16[256,1024]{1,0:T(8,128)(2,1)} %get-tuple-element.8), channel_id=1, source_target_pairs={{0,8},{1,9},{2,10},{3,11},{4,12},{5,13},{6,14},{7,15},{8,0},{9,1},... | collective-permute-start | bytes 1572872 | tf_op jit(solution)/shard_map/ppermute | solution.py:27
  40.2 13.6 %copy-start.3 = (s32[512]{0:T(512)S(1)}, s32[512]{0:T(512)}, u32[]{:S(2)}) copy-start(s32[512]{0:T(512)} %param.16) | copy-start | bytes 6148
  41.6 7.6 %collective-permute-start.6 = (bf16[128,1024]{1,0:T(8,128)(2,1)S(1)}, bf16[128,1024]{1,0:T(8,128)(2,1)S(1)}, u32[]{:S(2)}, u32[]{:S(2)}) collective-permute-start(bf16[128,1024]{1,0:T(8,128)(2,1)S(1)} %slice.44), channel_id=1, source_target_pairs={{0,1},{1,0},{2,3},{3,2},{4,5},{5,4},{6,7},{7,6},{8,9},{9,8},{10,11... | collective-permute-start | bytes 786440 | tf_op jit(solution)/shard_map/ppermute | solution.py:27
  49.3 5.2 %collective-permute-start.7 = (bf16[32,1024]{1,0:T(8,128)(2,1)S(1)}, bf16[32,1024]{1,0:T(8,128)(2,1)S(1)}, u32[]{:S(2)}, u32[]{:S(2)}) collective-permute-start(bf16[32,1024]{1,0:T(8,128)(2,1)S(1)} %get-tuple-element.11), channel_id=1, source_target_pairs={{0,2},{1,3},{2,0},{3,1},{4,6},{5,7},{6,4},{7,5},{8,10},{9,11},{10,... | collective-permute-start | bytes 196616 | tf_op jit(solution)/shard_map/ppermute | solution.py:27
  49.8 4.7 %collective-permute-start.8 = (bf16[32,1024]{1,0:T(8,128)(2,1)S(1)}, bf16[32,1024]{1,0:T(8,128)(2,1)S(1)}, u32[]{:S(2)}, u32[]{:S(2)}) collective-permute-start(bf16[32,1024]{1,0:T(8,128)(2,1)S(1)} %get-tuple-element.13), channel_id=1, source_target_pairs={{0,4},{1,5},{2,6},{3,7},{4,0},{5,1},{6,2},{7,3},{8,12},{9,13},{10,... | collective-permute-start | bytes 196616 | tf_op jit(solution)/shard_map/ppermute | solution.py:27
  51.2 5.7 %collective-permute-start.9 = (bf16[32,1024]{1,0:T(8,128)(2,1)S(1)}, bf16[32,1024]{1,0:T(8,128)(2,1)S(1)}, u32[]{:S(2)}, u32[]{:S(2)}) collective-permute-start(bf16[32,1024]{1,0:T(8,128)(2,1)S(1)} %get-tuple-element.12), channel_id=1, source_target_pairs={{0,6},{1,7},{2,4},{3,5},{4,2},{5,3},{6,0},{7,1},{8,14},{9,15},{10,... | collective-permute-start | bytes 196616 | tf_op jit(solution)/shard_map/ppermute | solution.py:27
  59.8 4.3 %collective-permute-start.10 = (bf16[32,128]{1,0:T(8,128)(2,1)}, bf16[32,128]{1,0:T(8,128)(2,1)S(1)}, u32[]{:S(2)}, u32[]{:S(2)}) collective-permute-start(bf16[32,128]{1,0:T(8,128)(2,1)} %shard_map.102), channel_id=1, source_target_pairs={{0,2},{1,3},{2,0},{3,1},{4,6},{5,7},{6,4},{7,5},{8,10},{9,11},{10,... | collective-permute-start | bytes 24584 | tf_op jit(solution)/shard_map/ppermute | solution.py:27
  60.5 3.6 %collective-permute-start.11 = (bf16[32,128]{1,0:T(8,128)(2,1)}, bf16[32,128]{1,0:T(8,128)(2,1)S(1)}, u32[]{:S(2)}, u32[]{:S(2)}) collective-permute-start(bf16[32,128]{1,0:T(8,128)(2,1)} %shard_map.102), channel_id=1, source_target_pairs={{0,4},{1,5},{2,6},{3,7},{4,0},{5,1},{6,2},{7,3},{8,12},{9,13},{10,... | collective-permute-start | bytes 24584 | tf_op jit(solution)/shard_map/ppermute | solution.py:27
  61.6 4.5 %collective-permute-start.12 = (bf16[32,128]{1,0:T(8,128)(2,1)}, bf16[32,128]{1,0:T(8,128)(2,1)S(1)}, u32[]{:S(2)}, u32[]{:S(2)}) collective-permute-start(bf16[32,128]{1,0:T(8,128)(2,1)} %shard_map.102), channel_id=1, source_target_pairs={{0,6},{1,7},{2,4},{3,5},{4,2},{5,3},{6,0},{7,1},{8,14},{9,15},{10,... | collective-permute-start | bytes 24584 | tf_op jit(solution)/shard_map/ppermute | solution.py:27
  66.8 3.1 %collective-permute-start.13 = (bf16[128,128]{1,0:T(8,128)(2,1)S(1)}, bf16[128,128]{1,0:T(8,128)(2,1)S(1)}, u32[]{:S(2)}, u32[]{:S(2)}) collective-permute-start(bf16[128,128]{1,0:T(8,128)(2,1)S(1)} %pad_maximum_fusion.2), channel_id=1, source_target_pairs={{0,1},{1,0},{2,3},{3,2},{4,5},{5,4},{6,7},{7,6},{8,9},{9,8},{10,11... | collective-permute-start | bytes 98312 | tf_op jit(solution)/shard_map/ppermute | solution.py:27
  69.9 6.4 %collective-permute-start.14 = (bf16[256,128]{1,0:T(8,128)(2,1)S(1)}, bf16[256,128]{1,0:T(8,128)(2,1)S(1)}, u32[]{:S(2)}, u32[]{:S(2)}) collective-permute-start(bf16[256,128]{1,0:T(8,128)(2,1)S(1)} %get-tuple-element.24), channel_id=1, source_target_pairs={{0,8},{1,9},{2,10},{3,11},{4,12},{5,13},{6,14},{7,15},{8,0},{9,1},... | collective-permute-start | bytes 196616 | tf_op jit(solution)/shard_map/ppermute | solution.py:27
  76.3 2.0 %copy-start = (bf16[512,128]{1,0:T(8,128)(2,1)}, bf16[512,128]{1,0:T(8,128)(2,1)S(1)}, u32[]{:S(2)}) copy-start(bf16[512,128]{1,0:T(8,128)(2,1)S(1)} %constant_dynamic-update-slice_fusion.16.q_ref) | copy-start | bytes 393220
